TPU v7x, 512 devices: a whole 4x8x8 slice. The times are simulated.
512 devices in a mesh: sims: 32 (over z_lo, y, core), sites: 16 (over x, z_hi).
Axes of the slice: x: 4, y: 8, z: 8 (z_hi: 4, z_lo: 2; z = z_hi * 2 + z_lo), core: 2. Of those that a mesh axis runs over, the one named last changes fastest.
Arguments:
- genotypes: int32 [32, 64, 8192], P('sims', None, 'sites'), may hold values from 0 to 1
- key_prior: bfloat16 [32, 2048], P('sims', 'sites'), may hold values from -300 to 300
- band_reach: int32 [32], P('sims'), may hold values from 128 to 512, as said below
- cotangent: bfloat16 [32, 2048, 512], P('sims', 'sites'), may hold values from -0.09375 to 0.09375
- conv_weight: float32 [4, 64], replicated, may hold values from -3 to 3
- conv_bias: float32 [64], replicated, may hold values from -3 to 3
- mix_weight: float32 [3, 64, 64], replicated, may hold values from -0.4375 to 0.4375
- embed_weight: float32 [64, 512], replicated, may hold values from -0.75 to 0.75
- norm_gain: float32 [512], replicated, may hold values from 0.5 to 1.5
- attn_weight: bfloat16 [4, 512, 512], replicated, may hold values from -0.25 to 0.25
Outputs:
- grad_attention: float32 [1048576], P(('sims', 'sites'))
- grad_conv: float32 [4, 64], replicated
- grad_bias: float32 [64], replicated
- grad_mix: float32 [3, 64, 64], replicated
- grad_embed: float32 [64, 512], replicated
- grad_gain: float32 [512], replicated
Inputs may be any that keep to these rules, and one draw needn't show every extreme that they name: `band_reach`: some evolution has reach exactly 512 in every draw.
All inputs are finite; a program needn't handle non-finite values.
Results may differ from a plain program's by a relative error of at most 0.017.
Values may be sent and summed in bfloat16 or wider, within the bound.
A program may use at most 64 MiB of HBM per device.

v0:
```python
import jax
import jax.numpy as jnp
from jax import lax
from jax.sharding import PartitionSpec as P

HEADS = 8
HEAD_DIM = 64
BAND = 512
HIGH = lax.Precision.HIGHEST
EPS = 1e-06


def extended(cells, sides, width):
    for axis, dim in sides:
        count = lax.axis_size(axis)
        head = lax.slice_in_dim(cells, 0, width, axis=dim)
        tail = lax.slice_in_dim(cells, cells.shape[dim] - width, cells.shape[dim], axis=dim)
        cells = jnp.concatenate(
            [
                lax.ppermute(tail, axis, [(i, (i + 1) % count) for i in range(count)]),
                cells,
                lax.ppermute(head, axis, [((i + 1) % count, i) for i in range(count)]),
            ],
            axis=dim,
        )
    return cells


def from_behind(value, axis, steps):
    count = lax.axis_size(axis)
    pairs = [(source, (source + steps) % count) for source in range(count)]
    return lax.ppermute(value, axis, pairs)


def silu_slope(value):
    sigma = jax.nn.sigmoid(value)
    return sigma * (1.0 + value * (1.0 - sigma))


def block_offsets(count, reach_blocks):
    chosen = []
    taken = []
    for distance in range(reach_blocks + 1):
        for offset in (distance, -distance):
            if offset % count not in taken:
                taken.append(offset % count)
                chosen.append(offset)
    return chosen


def split_heads(array, heads):
    return array.reshape(array.shape[0], array.shape[1], heads, array.shape[2] // heads)


def band_scores(query, keys, prior, query_places, key_places, limit, cycle_tokens, factor):
    scores = jnp.einsum("sqhe,skhe->shqk", query, keys, preferred_element_type=jnp.float32) * factor
    scores = scores + prior.astype(jnp.float32)[:, None, None, :]
    apart = (key_places[None, :] - query_places[:, None]) % cycle_tokens
    apart = jnp.minimum(apart, cycle_tokens - apart)
    inside = apart[None, None] <= limit[:, None, None, None]
    return (scores, inside)


def per_device(
    genotypes,
    key_prior,
    band_reach,
    cotangent,
    conv_weight,
    conv_bias,
    mix_weight,
    embed_weight,
    norm_gain,
    attn_weight,
):
    sims, haps, sites = genotypes.shape
    patch = conv_weight.shape[0]
    local = sites // patch
    width = attn_weight.shape[1]
    heads = HEADS
    factor = HEAD_DIM ** (-0.5)
    count = lax.axis_size("sites")
    cycle_tokens = local * count
    place = lax.axis_index("sites")
    ordinal = jnp.arange(local, dtype=jnp.int32)
    patches = genotypes.astype(jnp.float32).reshape(sims, haps, local, patch)
    pre = (
        jnp.einsum("shtk,kc->shct", patches, conv_weight, precision=HIGH)
        + conv_bias[None, None, :, None]
    )
    pooled = jnp.mean(jax.nn.silu(pre), axis=1)
    pooled_wide = extended(pooled, (("sites", 2),), 1)
    mixed = jnp.zeros((sims, mix_weight.shape[2], local), jnp.float32)
    for shift_by in (-1, 0, 1):
        mixed = mixed + jnp.einsum(
            "co,sct->sot",
            mix_weight[shift_by + 1],
            pooled_wide[:, :, 1 + shift_by : 1 + shift_by + local],
            precision=HIGH,
        )
    activated = jax.nn.silu(mixed)
    embedded = jnp.einsum("sct,cd->std", activated, embed_weight, precision=HIGH).astype(
        jnp.bfloat16
    )
    wide = embedded.astype(jnp.float32)
    inverse = lax.rsqrt(jnp.mean(wide * wide, axis=2, keepdims=True) + EPS)
    normed = (wide * inverse * norm_gain).astype(jnp.bfloat16)
    query = jnp.einsum(
        "std,de->ste", normed, attn_weight[0], preferred_element_type=jnp.float32
    ).astype(jnp.bfloat16)
    keys = jnp.einsum(
        "std,de->ste", normed, attn_weight[1], preferred_element_type=jnp.float32
    ).astype(jnp.bfloat16)
    values = jnp.einsum(
        "std,de->ste", normed, attn_weight[2], preferred_element_type=jnp.float32
    ).astype(jnp.bfloat16)
    query_heads = split_heads(query, heads)
    key_heads = split_heads(keys, heads)
    value_heads = split_heads(values, heads)
    reach_blocks = -(-BAND // local)
    offsets = block_offsets(count, reach_blocks)
    packed = jnp.concatenate([keys, values, key_prior[:, :, None]], axis=2)
    gathered = {0: packed}
    for offset in offsets[1:]:
        gathered[offset] = from_behind(packed, "sites", -offset)
    packed_cat = jnp.concatenate([gathered[offset] for offset in offsets], axis=1)
    key_cat = split_heads(packed_cat[:, :, :width], heads)
    value_cat = split_heads(packed_cat[:, :, width : 2 * width], heads)
    prior_cat = packed_cat[:, :, 2 * width]
    key_places = jnp.concatenate([(place + offset) % count * local + ordinal for offset in offsets])
    query_places = place * local + ordinal
    scores, inside = band_scores(
        query_heads, key_cat, prior_cat, query_places, key_places, band_reach, cycle_tokens, factor
    )
    row_top = jnp.max(jnp.where(inside, scores, -jnp.inf), axis=-1, keepdims=True)
    lifted = jnp.where(inside, jnp.exp(scores - row_top), 0.0)
    row_total = jnp.sum(lifted, axis=-1, keepdims=True)
    prob = lifted / row_total
    prob_half = prob.astype(jnp.bfloat16)
    attended_full = jnp.einsum(
        "shqk,skhe->sqhe", prob_half, value_cat, preferred_element_type=jnp.float32
    )
    attended = attended_full.astype(jnp.bfloat16).reshape(sims, local, width)
    grad_attended = jnp.einsum(
        "std,ed->ste", cotangent, attn_weight[3], preferred_element_type=jnp.float32
    ).astype(jnp.bfloat16)
    grad_heads = split_heads(grad_attended, heads)
    delta = jnp.einsum("sqhe,sqhe->shq", grad_heads.astype(jnp.float32), attended_full)
    grad_prob = jnp.einsum(
        "sqhe,skhe->shqk", grad_heads, value_cat, preferred_element_type=jnp.float32
    )
    grad_scores = (prob * (grad_prob - delta[..., None]) * factor).astype(jnp.bfloat16)
    grad_query = jnp.einsum(
        "shqk,skhe->sqhe", grad_scores, key_cat, preferred_element_type=jnp.float32
    ).astype(jnp.bfloat16)
    grad_query = grad_query.reshape(sims, local, width)
    key_part = jnp.einsum(
        "shqk,sqhe->skhe", grad_scores, query_heads, preferred_element_type=jnp.float32
    )
    value_part = jnp.einsum(
        "shqk,sqhe->skhe", prob_half, grad_heads, preferred_element_type=jnp.float32
    )
    key_sum = key_part[:, 0:local]
    value_sum = value_part[:, 0:local]
    for position, offset in enumerate(offsets[1:], start=1):
        lower = position * local
        both = jnp.concatenate(
            [key_part[:, lower : lower + local], value_part[:, lower : lower + local]], axis=2
        ).astype(jnp.bfloat16)
        back = from_behind(both, "sites", offset).astype(jnp.float32)
        key_sum = key_sum + back[:, :, :heads]
        value_sum = value_sum + back[:, :, heads:]
    grad_keys = key_sum.astype(jnp.bfloat16).reshape(sims, local, width)
    grad_values = value_sum.astype(jnp.bfloat16).reshape(sims, local, width)
    term_query = jnp.einsum("std,ste->de", normed, grad_query, preferred_element_type=jnp.float32)
    term_keys = jnp.einsum("std,ste->de", normed, grad_keys, preferred_element_type=jnp.float32)
    term_values = jnp.einsum("std,ste->de", normed, grad_values, preferred_element_type=jnp.float32)
    term_output = jnp.einsum("std,ste->de", attended, cotangent, preferred_element_type=jnp.float32)
    flat_terms = jnp.stack([term_query, term_keys, term_values, term_output]).reshape(-1)
    grad_attention = lax.psum_scatter(
        lax.psum_scatter(flat_terms, "sims", scatter_dimension=0, tiled=True),
        "sites",
        scatter_dimension=0,
        tiled=True,
    )
    grad_normed = jnp.einsum(
        "ste,de->std", grad_query, attn_weight[0], preferred_element_type=jnp.float32
    )
    grad_normed = grad_normed + jnp.einsum(
        "ste,de->std", grad_keys, attn_weight[1], preferred_element_type=jnp.float32
    )
    grad_normed = grad_normed + jnp.einsum(
        "ste,de->std", grad_values, attn_weight[2], preferred_element_type=jnp.float32
    )
    term_gain = jnp.sum(grad_normed * wide * inverse, axis=(0, 1))
    scaled = grad_normed * norm_gain
    grad_embedded = (
        inverse * scaled - wide * inverse**3 * jnp.sum(scaled * wide, axis=2, keepdims=True) / width
    )
    grad_embedded = grad_embedded + cotangent.astype(jnp.float32)
    term_embed = jnp.einsum("sct,std->cd", activated, grad_embedded, precision=HIGH)
    grad_mixed = jnp.einsum(
        "std,od->sot", grad_embedded, embed_weight, precision=HIGH
    ) * silu_slope(mixed)
    mixed_wide = extended(grad_mixed.astype(jnp.bfloat16), (("sites", 2),), 1).astype(
        grad_mixed.dtype
    )
    mix_terms = []
    grad_pooled = jnp.zeros(pooled.shape, jnp.float32)
    for shift_by in (-1, 0, 1):
        mix_terms.append(
            jnp.einsum(
                "sct,sot->co",
                pooled_wide[:, :, 1 + shift_by : 1 + shift_by + local],
                grad_mixed,
                precision=HIGH,
            )
        )
        grad_pooled = grad_pooled + jnp.einsum(
            "co,sot->sct",
            mix_weight[shift_by + 1],
            mixed_wide[:, :, 1 - shift_by : 1 - shift_by + local],
            precision=HIGH,
        )
    grad_pre = (grad_pooled / haps)[:, None] * silu_slope(pre)
    term_conv = jnp.einsum("shtk,shct->kc", patches, grad_pre, precision=HIGH)
    term_bias = jnp.sum(grad_pre, axis=(0, 1, 3))
    small = (term_conv, term_bias, jnp.stack(mix_terms), term_embed, term_gain)
    flat_small = lax.psum(jnp.concatenate([t.reshape(-1) for t in small]), ("sims", "sites"))
    pieces = []
    lower = 0
    for t in small:
        pieces.append(flat_small[lower : lower + t.size].reshape(t.shape))
        lower += t.size
    grad_conv, grad_bias, grad_mix, grad_embed, grad_gain = pieces
    return (grad_attention, grad_conv, grad_bias, grad_mix, grad_embed, grad_gain)


def solution(mesh):
    placed = (
        P("sims", None, "sites"),
        P("sims", "sites"),
        P("sims"),
        P("sims", "sites", None),
        P(),
        P(),
        P(),
        P(),
        P(),
        P(),
    )
    return jax.shard_map(
        per_device,
        mesh=mesh,
        in_specs=placed,
        out_specs=(P(("sims", "sites")), P(), P(), P(), P(), P()),
        check_vma=False,
    )
```

profile of v0, /device:TPU:8, one launch (start us, length us, event | category | flops | bytes accessed | tf_op | source)
XLA Modules:
  0.0 869.0 jit_solution(17943417780981665908)
XLA Ops:
  8.5 4.5 fusion.16
  13.1 13.1 %collective-permute-start.1 = (f32[1,64,1]{2,1,0:T(8,128)S(1)}, f32[1,64,1]{2,1,0:T(8,128)S(1)}, u32[]{:S(2)}, u32[]{:S(2)}) collective-permute-start(f32[1,64,1]{2,1,0:T(8,128)S(1)} %get-tuple-element.31), channel_id=1, source_target_pairs={{1,0},{2,1},{3,2},{4,3},{5,4},{6,5},{7,6},{8,7},{9,8},{10,9},{11,1... | collective-permute-start | bytes 776 | tf_op jit(solution)/shard_map/ppermute | solution.py:22
  26.3 1.9 collective-permute-start
  30.2 6.0 collective-permute-done
  39.5 2.1 collective-permute-start.2
  42.0 4.6 collective-permute-start.3
  46.7 1.9 collective-permute-start.4
  48.6 7.8 collective-permute-start.5
  56.4 1.9 collective-permute-start.6
  58.7 9.6 %collective-permute-done.2 = bf16[1,128,1025]{2,1,0:T(8,128)(2,1)} collective-permute-done((bf16[1,128,1025]{2,1,0:T(8,128)(2,1)}, bf16[1,128,1025]{2,1,0:T(8,128)(2,1)}, u32[]{:S(2)}, u32[]{:S(2)}) %collective-permute-start.2) | collective-permute-done | bytes 262432 | tf_op jit(solution)/shard_map/ppermute | solution.py:32
  68.3 1.9 collective-permute-start.7
  70.2 1.7 constant_dynamic-update-slice_fusion.7
  71.9 2.8 collective-permute-start.8
  74.7 1.7 constant_dynamic-update-slice_fusion.6
  76.4 3.8 collective-permute-done.4
  80.3 15.8 %collective-permute-start.9 = (bf16[1,128,1025]{2,1,0:T(8,128)(2,1)}, bf16[1,128,1025]{2,1,0:T(8,128)(2,1)S(1)}, u32[]{:S(2)}, u32[]{:S(2)}) collective-permute-start(bf16[1,128,1025]{2,1,0:T(8,128)(2,1)} %get-tuple-element.28), channel_id=1, source_target_pairs={{0,4},{1,5},{2,6},{3,7},{4,8},{5,9},{6,10},{7,11},{8,12},{9,13},{1... | collective-permute-start | bytes 787208 | tf_op jit(solution)/shard_map/ppermute | solution.py:32
  96.1 1.7 constant_dynamic-update-slice_fusion.5
  97.8 1.7 constant_dynamic-update-slice_fusion.4
  99.5 1.7 constant_dynamic-update-slice_fusion.3
  103.6 2.8 fusion.114
  106.4 1.7 convert_reduce_fusion
  108.9 1.7 copy.41
  110.6 1.5 fusion.5
  112.1 1.8 fusion.119
  116.0 1.3 fusion.8
  118.3 6.1 collective-permute-start.10
  124.4 4.0 collective-permute-start.11
  128.5 4.2 collective-permute-start.12
  132.7 7.7 collective-permute-start.13
  140.4 1.9 collective-permute-start.14
  142.5 6.9 collective-permute-start.15
  149.4 2.3 collective-permute-start.16
  151.7 4.8 collective-permute-start.17
  158.2 2.1 collective-permute-done.13
  160.4 4.4 collective-permute-done.14
  166.6 3.1 copy.52
  170.0 1.3 copy-done.2
  174.2 9.6 %collective-permute-start.19 = (bf16[1,64,1]{2,1,0:T(8,128)(2,1)S(1)}, bf16[1,64,1]{2,1,0:T(8,128)(2,1)S(1)}, u32[]{:S(2)}, u32[]{:S(2)}) collective-permute-start(bf16[1,64,1]{2,1,0:T(8,128)(2,1)S(1)} %get-tuple-element.33), channel_id=1, source_target_pairs={{0,1},{1,2},{2,3},{3,4},{4,5},{5,6},{6,7},{7,8},{8,9},{9,10},{10,1... | collective-permute-start | bytes 392 | tf_op jit(solution)/shard_map/ppermute | solution.py:20
  184.0 1.9 collective-permute-start.18
  186.1 4.4 collective-permute-done.18
  190.8 2.4 fusion.30
  195.1 1.3 dynamic-slice
  197.0 225.5 %all-reduce.8.cloned.1.call-done = f32[1048576]{0:T(1024)} async-done(((f32[1048576]{0:T(1024)}), f32[1048576]{0:T(1024)}) %all-reduce.8.cloned.1.call-update) | async-done | bytes 4194320
  422.5 1.6 dynamic-slice.1
  426.0 267.0 %all-reduce.6.cloned.1.call-done = f32[45888]{0:T(1024)} async-done(((f32[45888]{0:T(1024)}), f32[45888]{0:T(1024)}) %all-reduce.6.cloned.1.call-update) | async-done | bytes 183568 | tf_op jit(solution)/shard_map/psum | solution.py:229
  697.7 1.3 slice.310
  700.2 161.0 %all-reduce.10.cloned.1.call-done = f32[32768]{0:T(1024)} async-done(((f32[32768]{0:T(1024)}), f32[32768]{0:T(1024)}) %all-reduce.10.cloned.1.call-update) | async-done | bytes 131088
  861.1 1.3 dynamic-slice.3
  (146 shorter events, 29.0 us)
Async XLA Ops:
  7.2 29.4 %copy-start = (f32[64,512]{1,0:T(8,128)S(1)}, f32[64,512]{1,0:T(8,128)}, u32[]{:S(2)}) copy-start(f32[64,512]{1,0:T(8,128)} %param.17) | copy-start | bytes 393220
  7.2 415.3 %all-reduce.8.cloned.1.call-start = ((), (), s32[]{:S(2)}) async-start(), calls=%async_computation.1 | async-start | bytes 8388608
  8.4 4.6 copy-start.7
  8.5 21.1 %copy-start.5 = (f32[3,64,64]{2,1,0:T(8,128)S(1)}, f32[3,64,64]{2,1,0:T(8,128)}, u32[]{:S(2)}) copy-start(f32[3,64,64]{2,1,0:T(8,128)} %param.16) | copy-start | bytes 147460
  8.5 21.4 %copy-start.15 = (bf16[1,128]{1,0:T(2,128)(2,1)S(1)}, bf16[1,128]{1,0:T(2,128)(2,1)}, u32[]{:S(2)}) copy-start(bf16[1,128]{1,0:T(2,128)(2,1)} %param.11) | copy-start | bytes 772
  8.5 29.1 %copy-start.11 = (f32[512]{0:T(512)S(1)}, f32[512]{0:T(512)}, u32[]{:S(2)}) copy-start(f32[512]{0:T(512)} %param.18) | copy-start | bytes 6148
  8.5 29.6 %copy-start.1 = (bf16[4,512,512]{2,1,0:T(8,128)(2,1)S(1)}, bf16[4,512,512]{2,1,0:T(8,128)(2,1)}, u32[]{:S(2)}) copy-start(bf16[4,512,512]{2,1,0:T(8,128)(2,1)} %param.19) | copy-start | bytes 6291460
  13.1 28.5 %copy-start.4 = (bf16[1,128,512]{2,1,0:T(8,128)(2,1)S(1)}, bf16[1,128,512]{2,1,0:T(8,128)(2,1)}, u32[]{:S(2)}) copy-start(bf16[1,128,512]{2,1,0:T(8,128)(2,1)} %param.13) | copy-start | bytes 393220
  13.1 16.8 %collective-permute-start.1 = (f32[1,64,1]{2,1,0:T(8,128)S(1)}, f32[1,64,1]{2,1,0:T(8,128)S(1)}, u32[]{:S(2)}, u32[]{:S(2)}) collective-permute-start(f32[1,64,1]{2,1,0:T(8,128)S(1)} %get-tuple-element.31), channel_id=1, source_target_pairs={{1,0},{2,1},{3,2},{4,3},{5,4},{6,5},{7,6},{8,7},{9,8},{10,9},{11,1... | collective-permute-start | bytes 776 | tf_op jit(solution)/shard_map/ppermute | solution.py:22
  26.3 10.0 %collective-permute-start = (f32[1,64,1]{2,1,0:T(8,128)S(1)}, f32[1,64,1]{2,1,0:T(8,128)S(1)}, u32[]{:S(2)}, u32[]{:S(2)}) collective-permute-start(f32[1,64,1]{2,1,0:T(8,128)S(1)} %get-tuple-element.30), channel_id=1, source_target_pairs={{0,1},{1,2},{2,3},{3,4},{4,5},{5,6},{6,7},{7,8},{8,9},{9,10},{10,1... | collective-permute-start | bytes 776 | tf_op jit(solution)/shard_map/ppermute | solution.py:20
  36.3 1.4 copy-start.9
  37.6 0.5 copy-start.13
  39.5 28.8 %collective-permute-start.2 = (bf16[1,128,1025]{2,1,0:T(8,128)(2,1)}, bf16[1,128,1025]{2,1,0:T(8,128)(2,1)}, u32[]{:S(2)}, u32[]{:S(2)}) collective-permute-start(bf16[1,128,1025]{2,1,0:T(8,128)(2,1)} %get-tuple-element.28), channel_id=1, source_target_pairs={{0,15},{1,0},{2,1},{3,2},{4,3},{5,4},{6,5},{7,6},{8,7},{9,8},{10,9... | collective-permute-start | bytes 787208 | tf_op jit(solution)/shard_map/ppermute | solution.py:32
  42.0 29.9 %collective-permute-start.3 = (bf16[1,128,1025]{2,1,0:T(8,128)(2,1)}, bf16[1,128,1025]{2,1,0:T(8,128)(2,1)}, u32[]{:S(2)}, u32[]{:S(2)}) collective-permute-start(bf16[1,128,1025]{2,1,0:T(8,128)(2,1)} %get-tuple-element.28), channel_id=1, source_target_pairs={{0,1},{1,2},{2,3},{3,4},{4,5},{5,6},{6,7},{7,8},{8,9},{9,10},{10,1... | collective-permute-start | bytes 787208 | tf_op jit(solution)/shard_map/ppermute | solution.py:32
  46.7 33.6 %collective-permute-start.4 = (bf16[1,128,1025]{2,1,0:T(8,128)(2,1)}, bf16[1,128,1025]{2,1,0:T(8,128)(2,1)}, u32[]{:S(2)}, u32[]{:S(2)}) collective-permute-start(bf16[1,128,1025]{2,1,0:T(8,128)(2,1)} %get-tuple-element.28), channel_id=1, source_target_pairs={{0,14},{1,15},{2,0},{3,1},{4,2},{5,3},{6,4},{7,5},{8,6},{9,7},{10,... | collective-permute-start | bytes 787208 | tf_op jit(solution)/shard_map/ppermute | solution.py:32
  48.6 49.2 %collective-permute-start.5 = (bf16[1,128,1025]{2,1,0:T(8,128)(2,1)}, bf16[1,128,1025]{2,1,0:T(8,128)(2,1)}, u32[]{:S(2)}, u32[]{:S(2)}) collective-permute-start(bf16[1,128,1025]{2,1,0:T(8,128)(2,1)} %get-tuple-element.28), channel_id=1, source_target_pairs={{0,2},{1,3},{2,4},{3,5},{4,6},{5,7},{6,8},{7,9},{8,10},{9,11},{10,... | collective-permute-start | bytes 787208 | tf_op jit(solution)/shard_map/ppermute | solution.py:32
  56.4 43.0 %collective-permute-start.6 = (bf16[1,128,1025]{2,1,0:T(8,128)(2,1)}, bf16[1,128,1025]{2,1,0:T(8,128)(2,1)}, u32[]{:S(2)}, u32[]{:S(2)}) collective-permute-start(bf16[1,128,1025]{2,1,0:T(8,128)(2,1)} %get-tuple-element.28), channel_id=1, source_target_pairs={{0,13},{1,14},{2,15},{3,0},{4,1},{5,2},{6,3},{7,4},{8,5},{9,6},{10... | collective-permute-start | bytes 787208 | tf_op jit(solution)/shard_map/ppermute | solution.py:32
  68.3 32.9 %collective-permute-start.7 = (bf16[1,128,1025]{2,1,0:T(8,128)(2,1)}, bf16[1,128,1025]{2,1,0:T(8,128)(2,1)S(1)}, u32[]{:S(2)}, u32[]{:S(2)}) collective-permute-start(bf16[1,128,1025]{2,1,0:T(8,128)(2,1)} %get-tuple-element.28), channel_id=1, source_target_pairs={{0,3},{1,4},{2,5},{3,6},{4,7},{5,8},{6,9},{7,10},{8,11},{9,12},{10... | collective-permute-start | bytes 787208 | tf_op jit(solution)/shard_map/ppermute | solution.py:32
  71.9 30.0 %collective-permute-start.8 = (bf16[1,128,1025]{2,1,0:T(8,128)(2,1)}, bf16[1,128,1025]{2,1,0:T(8,128)(2,1)S(1)}, u32[]{:S(2)}, u32[]{:S(2)}) collective-permute-start(bf16[1,128,1025]{2,1,0:T(8,128)(2,1)} %get-tuple-element.28), channel_id=1, source_target_pairs={{0,12},{1,13},{2,14},{3,15},{4,0},{5,1},{6,2},{7,3},{8,4},{9,5},{1... | collective-permute-start | bytes 787208 | tf_op jit(solution)/shard_map/ppermute | solution.py:32
  80.3 22.6 %collective-permute-start.9 = (bf16[1,128,1025]{2,1,0:T(8,128)(2,1)}, bf16[1,128,1025]{2,1,0:T(8,128)(2,1)S(1)}, u32[]{:S(2)}, u32[]{:S(2)}) collective-permute-start(bf16[1,128,1025]{2,1,0:T(8,128)(2,1)} %get-tuple-element.28), channel_id=1, source_target_pairs={{0,4},{1,5},{2,6},{3,7},{4,8},{5,9},{6,10},{7,11},{8,12},{9,13},{1... | collective-permute-start | bytes 787208 | tf_op jit(solution)/shard_map/ppermute | solution.py:32
  118.3 24.1 %collective-permute-start.10 = (bf16[1,128,16,64]{1,3,2,0:T(8,128)(2,1)S(1)}, bf16[1,128,16,64]{1,3,2,0:T(8,128)(2,1)S(1)}, u32[]{:S(2)}, u32[]{:S(2)}) collective-permute-start(bf16[1,128,16,64]{1,3,2,0:T(8,128)(2,1)S(1)} %pad_maximum_fusion.2), channel_id=1, source_target_pairs={{0,1},{1,2},{2,3},{3,4},{4,5},{5,6},{6,7},{7,8},{8,9},{9,10},{10,1... | collective-permute-start | bytes 786440 | tf_op jit(solution)/shard_map/ppermute | solution.py:32
  124.4 25.0 %collective-permute-start.11 = (bf16[1,128,16,64]{1,3,2,0:T(8,128)(2,1)S(1)}, bf16[1,128,16,64]{1,3,2,0:T(8,128)(2,1)S(1)}, u32[]{:S(2)}, u32[]{:S(2)}) collective-permute-start(bf16[1,128,16,64]{1,3,2,0:T(8,128)(2,1)S(1)} %pad_maximum_fusion.3), channel_id=1, source_target_pairs={{0,15},{1,0},{2,1},{3,2},{4,3},{5,4},{6,5},{7,6},{8,7},{9,8},{10,9... | collective-permute-start | bytes 786440 | tf_op jit(solution)/shard_map/ppermute | solution.py:32
  128.5 23.2 %collective-permute-start.12 = (bf16[1,128,16,64]{1,3,2,0:T(8,128)(2,1)S(1)}, bf16[1,128,16,64]{1,3,2,0:T(8,128)(2,1)S(1)}, u32[]{:S(2)}, u32[]{:S(2)}) collective-permute-start(bf16[1,128,16,64]{1,3,2,0:T(8,128)(2,1)S(1)} %pad_maximum_fusion.4), channel_id=1, source_target_pairs={{0,2},{1,3},{2,4},{3,5},{4,6},{5,7},{6,8},{7,9},{8,10},{9,11},{10,... | collective-permute-start | bytes 786440 | tf_op jit(solution)/shard_map/ppermute | solution.py:32
  132.7 27.7 %collective-permute-start.13 = (bf16[1,128,16,64]{1,3,2,0:T(8,128)(2,1)S(1)}, bf16[1,128,16,64]{1,3,2,0:T(8,128)(2,1)S(1)}, u32[]{:S(2)}, u32[]{:S(2)}) collective-permute-start(bf16[1,128,16,64]{1,3,2,0:T(8,128)(2,1)S(1)} %pad_maximum_fusion.5), channel_id=1, source_target_pairs={{0,14},{1,15},{2,0},{3,1},{4,2},{5,3},{6,4},{7,5},{8,6},{9,7},{10,... | collective-permute-start | bytes 786440 | tf_op jit(solution)/shard_map/ppermute | solution.py:32
  140.4 24.4 %collective-permute-start.14 = (bf16[1,128,16,64]{1,3,2,0:T(8,128)(2,1)S(1)}, bf16[1,128,16,64]{1,3,2,0:T(8,128)(2,1)S(1)}, u32[]{:S(2)}, u32[]{:S(2)}) collective-permute-start(bf16[1,128,16,64]{1,3,2,0:T(8,128)(2,1)S(1)} %pad_maximum_fusion.6), channel_id=1, source_target_pairs={{0,3},{1,4},{2,5},{3,6},{4,7},{5,8},{6,9},{7,10},{8,11},{9,12},{10... | collective-permute-start | bytes 786440 | tf_op jit(solution)/shard_map/ppermute | solution.py:32
  142.5 22.4 %collective-permute-start.15 = (bf16[1,128,16,64]{1,3,2,0:T(8,128)(2,1)S(1)}, bf16[1,128,16,64]{1,3,2,0:T(8,128)(2,1)S(1)}, u32[]{:S(2)}, u32[]{:S(2)}) collective-permute-start(bf16[1,128,16,64]{1,3,2,0:T(8,128)(2,1)S(1)} %pad_maximum_fusion.7), channel_id=1, source_target_pairs={{0,13},{1,14},{2,15},{3,0},{4,1},{5,2},{6,3},{7,4},{8,5},{9,6},{10... | collective-permute-start | bytes 786440 | tf_op jit(solution)/shard_map/ppermute | solution.py:32
  149.4 15.5 %collective-permute-start.16 = (bf16[1,128,16,64]{1,3,2,0:T(8,128)(2,1)S(1)}, bf16[1,128,16,64]{1,3,2,0:T(8,128)(2,1)S(1)}, u32[]{:S(2)}, u32[]{:S(2)}) collective-permute-start(bf16[1,128,16,64]{1,3,2,0:T(8,128)(2,1)S(1)} %pad_maximum_fusion.8), channel_id=1, source_target_pairs={{0,4},{1,5},{2,6},{3,7},{4,8},{5,9},{6,10},{7,11},{8,12},{9,13},{1... | collective-permute-start | bytes 786440 | tf_op jit(solution)/shard_map/ppermute | solution.py:32
  151.7 13.2 %collective-permute-start.17 = (bf16[1,128,16,64]{1,3,2,0:T(8,128)(2,1)S(1)}, bf16[1,128,16,64]{1,3,2,0:T(8,128)(2,1)S(1)}, u32[]{:S(2)}, u32[]{:S(2)}) collective-permute-start(bf16[1,128,16,64]{1,3,2,0:T(8,128)(2,1)S(1)} %pad_maximum_fusion.9), channel_id=1, source_target_pairs={{0,12},{1,13},{2,14},{3,15},{4,0},{5,1},{6,2},{7,3},{8,4},{9,5},{1... | collective-permute-start | bytes 786440 | tf_op jit(solution)/shard_map/ppermute | solution.py:32
  169.7 1.6 copy-start.2
  169.7 2.2 copy-start.12
  169.7 2.2 copy-start.14
  169.7 2.7 copy-start.16
  169.8 523.3 %all-reduce.6.cloned.1.call-start = ((), (), s32[]{:S(2)}) async-start(), calls=%async_computation | async-start | bytes 368640 | tf_op jit(solution)/shard_map/psum | solution.py:229
  171.6 1.7 copy-start.10
  172.0 11.9 %copy-start.6 = (f32[3,64,64]{2,1,0:T(8,128)S(1)}, f32[3,64,64]{2,1,0:T(8,128)}, u32[]{:S(2)}) copy-start(f32[3,64,64]{2,1,0:T(8,128)} %param.16) | copy-start | bytes 147460
  172.0 18.8 %copy-start.8 = (f32[64,128,4]{1,2,0:T(4,128)S(1)}, f32[64,128,4]{1,2,0:T(4,128)}, u32[]{:S(2)}) copy-start(f32[64,128,4]{1,2,0:T(4,128)} %copy-done.7) | copy-start | bytes 393220
  172.0 18.8 %copy-start.17 = (f32[64]{0:T(128)S(1)}, f32[64]{0:T(128)}, u32[]{:S(2)}) copy-start(f32[64]{0:T(128)} %param.15) | copy-start | bytes 772
  172.4 18.3 %copy-start.3 = (f32[64,64,128]{2,0,1:T(8,128)S(1)}, f32[64,64,128]{2,0,1:T(8,128)}, u32[]{:S(2)}) copy-start(f32[64,64,128]{2,0,1:T(8,128)} %get-tuple-element.37) | copy-start | bytes 6291460
  174.2 11.7 %collective-permute-start.19 = (bf16[1,64,1]{2,1,0:T(8,128)(2,1)S(1)}, bf16[1,64,1]{2,1,0:T(8,128)(2,1)S(1)}, u32[]{:S(2)}, u32[]{:S(2)}) collective-permute-start(bf16[1,64,1]{2,1,0:T(8,128)(2,1)S(1)} %get-tuple-element.33), channel_id=1, source_target_pairs={{0,1},{1,2},{2,3},{3,4},{4,5},{5,6},{6,7},{7,8},{8,9},{9,10},{10,1... | collective-permute-start | bytes 392 | tf_op jit(solution)/shard_map/ppermute | solution.py:20
  184.0 6.5 collective-permute-start.18
  195.1 666.1 %all-reduce.10.cloned.1.call-start = ((), (), s32[]{:S(2)}) async-start(), calls=%async_computation.2 | async-start | bytes 262144
Sparse Core Ops, SparseCore 0:
  169.9 252.5 all-reduce.7
  427.5 265.5 all-reduce.5
  696.2 164.9 all-reduce.9
where the time goes:
time: 870 us; the launch traced here: 869 us
  waiting for transfers between devices  684 us (79%)
  starting transfers between devices  104 us (12%)
  local copies, waits for them, and re-layouts  35.6 us (4%)
  matrix products  19.2 us (2%)
  between operations  16.8 us (2%)
  other arithmetic  9.7 us (1%)
    unnamed x5, waiting for transfers between devices  386 us
    psum x1, waiting for transfers between devices, per_device(): lax.psum(jnp.concatenate([t.reshape(-1) for t in small]), ('sims', 'sites'))  267 us
    ppermute x16, starting transfers between devices, from_behind(): return lax.ppermute(value, axis, pairs)  76.7 us
    unnamed x49, local copies, waits for them, and re-layouts  20.3 us
    ppermute x16, waiting for transfers between devices, from_behind(): return lax.ppermute(value, axis, pairs)  20.2 us
  transfers between devices with their start and end apart: 23, of which 10 were waited for; matrix products, arithmetic and copies ran while one was open for 4% of the time, Pallas kernels for 0%

commit v1 on v0

--- a/solution.py
+++ b/solution.py
@@ -1,3 +1,4 @@
+import functools
 import jax
 import jax.numpy as jnp
 from jax import lax
@@ -8,6 +9,14 @@
 BAND = 512
 HIGH = lax.Precision.HIGHEST
 EPS = 1e-06
+
+
+def define_the_results(q_in, chip_axis, across):
+    current_block = lax.psum(q_in, chip_axis)
+    return lax.psum(current_block, across)
+
+
+extend_stacks_all_all = functools.partial(define_the_results, chip_axis="sims", across="sites")
 
 
 def extended(cells, sides, width):
@@ -226,7 +235,7 @@
     term_conv = jnp.einsum("shtk,shct->kc", patches, grad_pre, precision=HIGH)
     term_bias = jnp.sum(grad_pre, axis=(0, 1, 3))
     small = (term_conv, term_bias, jnp.stack(mix_terms), term_embed, term_gain)
-    flat_small = lax.psum(jnp.concatenate([t.reshape(-1) for t in small]), ("sims", "sites"))
+    flat_small = extend_stacks_all_all(jnp.concatenate([t.reshape(-1) for t in small]))
     pieces = []
     lower = 0
     for t in small:

time: 870 us -> 634 us (0.73)
  waiting for transfers between devices: 684 us -> 439 us
    psum x1 -> x0, waiting for transfers between devices: 267 us -> none  [per_device(): lax.psum(jnp.concatenate([t.reshape(-1) for t in small]), ('sims', 'sites'))]
    unnamed x5 -> x4, waiting for transfers between devices: 386 us -> 418 us
    unnamed x49 -> x51, local copies, waits for them, and re-layouts: 20.3 us -> 19.2 us
  transfers between devices with their start and end apart: 23 -> 22, of which waited for: 10 -> 8; matrix products, arithmetic and copies ran while one was open for 4% -> 3% of each run, Pallas kernels for 0% -> 0%
where the time goes in v1:
time: 634 us; the launch traced here: 632 us
  waiting for transfers between devices  439 us (69%)
  starting transfers between devices  110 us (17%)
  local copies, waits for them, and re-layouts  35.8 us (6%)
  matrix products  21.3 us (3%)
  between operations  17.1 us (3%)
  other arithmetic  9.77 us (2%)
    unnamed x4, waiting for transfers between devices  418 us
    ppermute x16, starting transfers between devices, from_behind(): return lax.ppermute(value, axis, pairs)  83.2 us
    unnamed x51, local copies, waits for them, and re-layouts  19.2 us
    ppermute x2, starting transfers between devices, extended(): lax.ppermute(head, axis, [((i + 1) % count, i) for i in range(count)])  15.3 us
    ppermute x16, waiting for transfers between devices, from_behind(): return lax.ppermute(value, axis, pairs)  14.6 us
  transfers between devices with their start and end apart: 22, of which 8 were waited for; matrix products, arithmetic and copies ran while one was open for 3% of the time, Pallas kernels for 0%

profile of v1, /device:TPU:8, one launch (start us, length us, event | category | flops | bytes accessed | tf_op | source)
XLA Modules:
  0.0 632.4 jit_solution(18063071305196378591)
XLA Ops:
  9.1 4.5 fusion.16
  13.7 13.1 %collective-permute-start.1 = (f32[1,64,1]{2,1,0:T(8,128)S(1)}, f32[1,64,1]{2,1,0:T(8,128)S(1)}, u32[]{:S(2)}, u32[]{:S(2)}) collective-permute-start(f32[1,64,1]{2,1,0:T(8,128)S(1)} %get-tuple-element.35), channel_id=1, source_target_pairs={{1,0},{2,1},{3,2},{4,3},{5,4},{6,5},{7,6},{8,7},{9,8},{10,9},{11,1... | collective-permute-start | bytes 776 | tf_op jit(solution)/shard_map/ppermute | solution.py:31
  26.9 1.9 collective-permute-start
  30.9 6.0 collective-permute-done
  39.1 2.1 collective-permute-start.2
  41.7 4.6 collective-permute-start.3
  46.3 1.9 collective-permute-start.4
  48.3 7.8 %collective-permute-start.5 = (bf16[1,128,1025]{2,1,0:T(8,128)(2,1)}, bf16[1,128,1025]{2,1,0:T(8,128)(2,1)}, u32[]{:S(2)}, u32[]{:S(2)}) collective-permute-start(bf16[1,128,1025]{2,1,0:T(8,128)(2,1)} %get-tuple-element.32), channel_id=1, source_target_pairs={{0,2},{1,3},{2,4},{3,5},{4,6},{5,7},{6,8},{7,9},{8,10},{9,11},{10,... | collective-permute-start | bytes 787208 | tf_op jit(solution)/shard_map/ppermute | solution.py:41
  56.1 1.9 collective-permute-start.6
  58.4 6.0 collective-permute-start.7
  64.5 1.7 constant_dynamic-update-slice_fusion.7
  66.2 3.6 collective-permute-done.3
  69.7 4.6 collective-permute-start.8
  74.3 1.7 constant_dynamic-update-slice_fusion.6
  76.0 3.6 collective-permute-done.4
  79.7 16.0 %collective-permute-start.9 = (bf16[1,128,1025]{2,1,0:T(8,128)(2,1)}, bf16[1,128,1025]{2,1,0:T(8,128)(2,1)S(1)}, u32[]{:S(2)}, u32[]{:S(2)}) collective-permute-start(bf16[1,128,1025]{2,1,0:T(8,128)(2,1)} %get-tuple-element.32), channel_id=1, source_target_pairs={{0,4},{1,5},{2,6},{3,7},{4,8},{5,9},{6,10},{7,11},{8,12},{9,13},{1... | collective-permute-start | bytes 787208 | tf_op jit(solution)/shard_map/ppermute | solution.py:41
  95.7 1.7 constant_dynamic-update-slice_fusion.5
  97.4 1.7 constant_dynamic-update-slice_fusion.4
  99.1 1.7 constant_dynamic-update-slice_fusion.3
  103.3 2.8 fusion.114
  108.0 1.7 copy.41
  110.5 1.8 fusion.119
  113.9 1.3 fusion.8
  117.7 6.1 collective-permute-start.10
  123.9 4.1 collective-permute-start.11
  128.0 4.2 collective-permute-start.12
  132.2 7.7 %collective-permute-start.13 = (bf16[1,128,16,64]{1,3,2,0:T(8,128)(2,1)S(1)}, bf16[1,128,16,64]{1,3,2,0:T(8,128)(2,1)S(1)}, u32[]{:S(2)}, u32[]{:S(2)}) collective-permute-start(bf16[1,128,16,64]{1,3,2,0:T(8,128)(2,1)S(1)} %pad_maximum_fusion.5), channel_id=1, source_target_pairs={{0,14},{1,15},{2,0},{3,1},{4,2},{5,3},{6,4},{7,5},{8,6},{9,7},{10,... | collective-permute-start | bytes 786440 | tf_op jit(solution)/shard_map/ppermute | solution.py:41
  140.0 2.1 collective-permute-start.14
  142.5 6.9 %collective-permute-start.15 = (bf16[1,128,16,64]{1,3,2,0:T(8,128)(2,1)S(1)}, bf16[1,128,16,64]{1,3,2,0:T(8,128)(2,1)S(1)}, u32[]{:S(2)}, u32[]{:S(2)}) collective-permute-start(bf16[1,128,16,64]{1,3,2,0:T(8,128)(2,1)S(1)} %pad_maximum_fusion.7), channel_id=1, source_target_pairs={{0,13},{1,14},{2,15},{3,0},{4,1},{5,2},{6,3},{7,4},{8,5},{9,6},{10... | collective-permute-start | bytes 786440 | tf_op jit(solution)/shard_map/ppermute | solution.py:41
  149.4 1.9 collective-permute-start.16
  151.4 5.1 collective-permute-start.17
  157.2 2.7 collective-permute-done.13
  160.0 4.5 collective-permute-done.14
  168.0 1.5 fusion.70
  169.8 1.3 convolution_bitcast_fusion.3
  172.6 9.4 %collective-permute-start.19 = (bf16[1,64,1]{2,1,0:T(8,128)(2,1)}, bf16[1,64,1]{2,1,0:T(8,128)(2,1)S(1)}, u32[]{:S(2)}, u32[]{:S(2)}) collective-permute-start(bf16[1,64,1]{2,1,0:T(8,128)(2,1)} %get-tuple-element.37), channel_id=1, source_target_pairs={{0,1},{1,2},{2,3},{3,4},{4,5},{5,6},{6,7},{7,8},{8,9},{9,10},{10,1... | collective-permute-start | bytes 392 | tf_op jit(solution)/shard_map/ppermute | solution.py:29
  182.0 2.1 collective-permute-start.18
  184.1 1.7 pad_maximum_fusion
  185.8 3.1 copy.52
  190.4 2.4 fusion.30
  193.8 1.3 dynamic-slice
  195.7 248.9 %all-reduce.7.cloned.1.call-done = (f32[1048576]{0:T(1024)}, f32[45888]{0:T(1024)}) async-done(((f32[1048576]{0:T(1024)}, f32[45888]{0:T(1024)}), (f32[1048576]{0:T(1024)}, f32[45888]{0:T(1024)})) %all-reduce.7.cloned.1.call-update) | async-done | bytes 4377872
  444.6 1.6 dynamic-slice.1
  446.2 1.3 dynamic-slice.2
  448.1 168.9 %all-reduce.9.cloned.1.call-done = (f32[32768]{0:T(1024)}, f32[45888]{0:T(1024)}) async-done(((f32[32768]{0:T(1024)}, f32[45888]{0:T(1024)}), (f32[32768]{0:T(1024)}, f32[45888]{0:T(1024)})) %all-reduce.9.cloned.1.call-update) | async-done | bytes 314640
  619.7 1.3 slice.310
  621.0 1.2 slice.307
  624.2 1.3 dynamic-slice.3
  (145 shorter events, 28.8 us)
Async XLA Ops:
  7.2 30.0 %copy-start = (f32[64,512]{1,0:T(8,128)S(1)}, f32[64,512]{1,0:T(8,128)}, u32[]{:S(2)}) copy-start(f32[64,512]{1,0:T(8,128)} %param.17) | copy-start | bytes 393220
  7.2 437.4 %all-reduce.7.cloned.1.call-start = ((), (), s32[]{:S(2)}) async-start(), calls=%async_computation | async-start | bytes 8757248
  8.4 0.7 copy-start.9
  9.1 21.1 %copy-start.6 = (f32[3,64,64]{2,1,0:T(8,128)S(1)}, f32[3,64,64]{2,1,0:T(8,128)}, u32[]{:S(2)}) copy-start(f32[3,64,64]{2,1,0:T(8,128)} %param.16) | copy-start | bytes 147460
  9.1 21.3 %copy-start.17 = (bf16[1,128]{1,0:T(2,128)(2,1)S(1)}, bf16[1,128]{1,0:T(2,128)(2,1)}, u32[]{:S(2)}) copy-start(bf16[1,128]{1,0:T(2,128)(2,1)} %param.11) | copy-start | bytes 772
  9.1 28.6 %copy-start.14 = (f32[512]{0:T(512)S(1)}, f32[512]{0:T(512)}, u32[]{:S(2)}) copy-start(f32[512]{0:T(512)} %param.18) | copy-start | bytes 6148
  9.1 28.7 %copy-start.1 = (bf16[4,512,512]{2,1,0:T(8,128)(2,1)S(1)}, bf16[4,512,512]{2,1,0:T(8,128)(2,1)}, u32[]{:S(2)}) copy-start(bf16[4,512,512]{2,1,0:T(8,128)(2,1)} %param.19) | copy-start | bytes 6291460
  13.6 27.6 %copy-start.4 = (bf16[1,128,512]{2,1,0:T(8,128)(2,1)S(1)}, bf16[1,128,512]{2,1,0:T(8,128)(2,1)}, u32[]{:S(2)}) copy-start(bf16[1,128,512]{2,1,0:T(8,128)(2,1)} %param.13) | copy-start | bytes 393220
  13.7 16.8 %collective-permute-start.1 = (f32[1,64,1]{2,1,0:T(8,128)S(1)}, f32[1,64,1]{2,1,0:T(8,128)S(1)}, u32[]{:S(2)}, u32[]{:S(2)}) collective-permute-start(f32[1,64,1]{2,1,0:T(8,128)S(1)} %get-tuple-element.35), channel_id=1, source_target_pairs={{1,0},{2,1},{3,2},{4,3},{5,4},{6,5},{7,6},{8,7},{9,8},{10,9},{11,1... | collective-permute-start | bytes 776 | tf_op jit(solution)/shard_map/ppermute | solution.py:31
  26.9 10.0 %collective-permute-start = (f32[1,64,1]{2,1,0:T(8,128)S(1)}, f32[1,64,1]{2,1,0:T(8,128)S(1)}, u32[]{:S(2)}, u32[]{:S(2)}) collective-permute-start(f32[1,64,1]{2,1,0:T(8,128)S(1)} %get-tuple-element.34), channel_id=1, source_target_pairs={{0,1},{1,2},{2,3},{3,4},{4,5},{5,6},{6,7},{7,8},{8,9},{9,10},{10,1... | collective-permute-start | bytes 776 | tf_op jit(solution)/shard_map/ppermute | solution.py:29
  36.9 21.1 %copy-start.12 = (f32[1,64,1]{2,1,0:T(8,128)}, f32[1,64,1]{2,1,0:T(8,128)S(1)}, u32[]{:S(2)}) copy-start(f32[1,64,1]{2,1,0:T(8,128)S(1)} %collective-permute-done) | copy-start | bytes 772
  39.1 19.3 %collective-permute-start.2 = (bf16[1,128,1025]{2,1,0:T(8,128)(2,1)}, bf16[1,128,1025]{2,1,0:T(8,128)(2,1)}, u32[]{:S(2)}, u32[]{:S(2)}) collective-permute-start(bf16[1,128,1025]{2,1,0:T(8,128)(2,1)} %get-tuple-element.32), channel_id=1, source_target_pairs={{0,15},{1,0},{2,1},{3,2},{4,3},{5,4},{6,5},{7,6},{8,7},{9,8},{10,9... | collective-permute-start | bytes 787208 | tf_op jit(solution)/shard_map/ppermute | solution.py:41
  41.7 28.0 %collective-permute-start.3 = (bf16[1,128,1025]{2,1,0:T(8,128)(2,1)}, bf16[1,128,1025]{2,1,0:T(8,128)(2,1)}, u32[]{:S(2)}, u32[]{:S(2)}) collective-permute-start(bf16[1,128,1025]{2,1,0:T(8,128)(2,1)} %get-tuple-element.32), channel_id=1, source_target_pairs={{0,1},{1,2},{2,3},{3,4},{4,5},{5,6},{6,7},{7,8},{8,9},{9,10},{10,1... | collective-permute-start | bytes 787208 | tf_op jit(solution)/shard_map/ppermute | solution.py:41
  46.3 33.3 %collective-permute-start.4 = (bf16[1,128,1025]{2,1,0:T(8,128)(2,1)}, bf16[1,128,1025]{2,1,0:T(8,128)(2,1)}, u32[]{:S(2)}, u32[]{:S(2)}) collective-permute-start(bf16[1,128,1025]{2,1,0:T(8,128)(2,1)} %get-tuple-element.32), channel_id=1, source_target_pairs={{0,14},{1,15},{2,0},{3,1},{4,2},{5,3},{6,4},{7,5},{8,6},{9,7},{10,... | collective-permute-start | bytes 787208 | tf_op jit(solution)/shard_map/ppermute | solution.py:41
  48.3 49.2 %collective-permute-start.5 = (bf16[1,128,1025]{2,1,0:T(8,128)(2,1)}, bf16[1,128,1025]{2,1,0:T(8,128)(2,1)}, u32[]{:S(2)}, u32[]{:S(2)}) collective-permute-start(bf16[1,128,1025]{2,1,0:T(8,128)(2,1)} %get-tuple-element.32), channel_id=1, source_target_pairs={{0,2},{1,3},{2,4},{3,5},{4,6},{5,7},{6,8},{7,9},{8,10},{9,11},{10,... | collective-permute-start | bytes 787208 | tf_op jit(solution)/shard_map/ppermute | solution.py:41
  56.1 43.0 %collective-permute-start.6 = (bf16[1,128,1025]{2,1,0:T(8,128)(2,1)}, bf16[1,128,1025]{2,1,0:T(8,128)(2,1)}, u32[]{:S(2)}, u32[]{:S(2)}) collective-permute-start(bf16[1,128,1025]{2,1,0:T(8,128)(2,1)} %get-tuple-element.32), channel_id=1, source_target_pairs={{0,13},{1,14},{2,15},{3,0},{4,1},{5,2},{6,3},{7,4},{8,5},{9,6},{10... | collective-permute-start | bytes 787208 | tf_op jit(solution)/shard_map/ppermute | solution.py:41
  58.4 42.4 %collective-permute-start.7 = (bf16[1,128,1025]{2,1,0:T(8,128)(2,1)}, bf16[1,128,1025]{2,1,0:T(8,128)(2,1)S(1)}, u32[]{:S(2)}, u32[]{:S(2)}) collective-permute-start(bf16[1,128,1025]{2,1,0:T(8,128)(2,1)} %get-tuple-element.32), channel_id=1, source_target_pairs={{0,3},{1,4},{2,5},{3,6},{4,7},{5,8},{6,9},{7,10},{8,11},{9,12},{10... | collective-permute-start | bytes 787208 | tf_op jit(solution)/shard_map/ppermute | solution.py:41
  69.7 31.9 %collective-permute-start.8 = (bf16[1,128,1025]{2,1,0:T(8,128)(2,1)}, bf16[1,128,1025]{2,1,0:T(8,128)(2,1)S(1)}, u32[]{:S(2)}, u32[]{:S(2)}) collective-permute-start(bf16[1,128,1025]{2,1,0:T(8,128)(2,1)} %get-tuple-element.32), channel_id=1, source_target_pairs={{0,12},{1,13},{2,14},{3,15},{4,0},{5,1},{6,2},{7,3},{8,4},{9,5},{1... | collective-permute-start | bytes 787208 | tf_op jit(solution)/shard_map/ppermute | solution.py:41
  79.7 22.9 %collective-permute-start.9 = (bf16[1,128,1025]{2,1,0:T(8,128)(2,1)}, bf16[1,128,1025]{2,1,0:T(8,128)(2,1)S(1)}, u32[]{:S(2)}, u32[]{:S(2)}) collective-permute-start(bf16[1,128,1025]{2,1,0:T(8,128)(2,1)} %get-tuple-element.32), channel_id=1, source_target_pairs={{0,4},{1,5},{2,6},{3,7},{4,8},{5,9},{6,10},{7,11},{8,12},{9,13},{1... | collective-permute-start | bytes 787208 | tf_op jit(solution)/shard_map/ppermute | solution.py:41
  117.7 24.7 %collective-permute-start.10 = (bf16[1,128,16,64]{1,3,2,0:T(8,128)(2,1)S(1)}, bf16[1,128,16,64]{1,3,2,0:T(8,128)(2,1)S(1)}, u32[]{:S(2)}, u32[]{:S(2)}) collective-permute-start(bf16[1,128,16,64]{1,3,2,0:T(8,128)(2,1)S(1)} %pad_maximum_fusion.2), channel_id=1, source_target_pairs={{0,1},{1,2},{2,3},{3,4},{4,5},{5,6},{6,7},{7,8},{8,9},{9,10},{10,1... | collective-permute-start | bytes 786440 | tf_op jit(solution)/shard_map/ppermute | solution.py:41
  123.8 32.7 %copy-start.5 = (bf16[1,128,512]{2,1,0:T(8,128)(2,1)S(1)}, bf16[1,128,512]{2,1,0:T(8,128)(2,1)}, u32[]{:S(2)}) copy-start(bf16[1,128,512]{2,1,0:T(8,128)(2,1)} %param.13) | copy-start | bytes 393220
  123.9 25.6 %collective-permute-start.11 = (bf16[1,128,16,64]{1,3,2,0:T(8,128)(2,1)S(1)}, bf16[1,128,16,64]{1,3,2,0:T(8,128)(2,1)S(1)}, u32[]{:S(2)}, u32[]{:S(2)}) collective-permute-start(bf16[1,128,16,64]{1,3,2,0:T(8,128)(2,1)S(1)} %pad_maximum_fusion.3), channel_id=1, source_target_pairs={{0,15},{1,0},{2,1},{3,2},{4,3},{5,4},{6,5},{7,6},{8,7},{9,8},{10,9... | collective-permute-start | bytes 786440 | tf_op jit(solution)/shard_map/ppermute | solution.py:41
  128.0 23.3 %collective-permute-start.12 = (bf16[1,128,16,64]{1,3,2,0:T(8,128)(2,1)S(1)}, bf16[1,128,16,64]{1,3,2,0:T(8,128)(2,1)S(1)}, u32[]{:S(2)}, u32[]{:S(2)}) collective-permute-start(bf16[1,128,16,64]{1,3,2,0:T(8,128)(2,1)S(1)} %pad_maximum_fusion.4), channel_id=1, source_target_pairs={{0,2},{1,3},{2,4},{3,5},{4,6},{5,7},{6,8},{7,9},{8,10},{9,11},{10,... | collective-permute-start | bytes 786440 | tf_op jit(solution)/shard_map/ppermute | solution.py:41
  132.2 27.7 %collective-permute-start.13 = (bf16[1,128,16,64]{1,3,2,0:T(8,128)(2,1)S(1)}, bf16[1,128,16,64]{1,3,2,0:T(8,128)(2,1)S(1)}, u32[]{:S(2)}, u32[]{:S(2)}) collective-permute-start(bf16[1,128,16,64]{1,3,2,0:T(8,128)(2,1)S(1)} %pad_maximum_fusion.5), channel_id=1, source_target_pairs={{0,14},{1,15},{2,0},{3,1},{4,2},{5,3},{6,4},{7,5},{8,6},{9,7},{10,... | collective-permute-start | bytes 786440 | tf_op jit(solution)/shard_map/ppermute | solution.py:41
  139.9 16.9 %copy-start.2 = (bf16[4,512,512]{2,1,0:T(8,128)(2,1)S(1)}, bf16[4,512,512]{2,1,0:T(8,128)(2,1)}, u32[]{:S(2)}) copy-start(bf16[4,512,512]{2,1,0:T(8,128)(2,1)} %param.19) | copy-start | bytes 6291460
  140.0 24.5 %collective-permute-start.14 = (bf16[1,128,16,64]{1,3,2,0:T(8,128)(2,1)S(1)}, bf16[1,128,16,64]{1,3,2,0:T(8,128)(2,1)S(1)}, u32[]{:S(2)}, u32[]{:S(2)}) collective-permute-start(bf16[1,128,16,64]{1,3,2,0:T(8,128)(2,1)S(1)} %pad_maximum_fusion.6), channel_id=1, source_target_pairs={{0,3},{1,4},{2,5},{3,6},{4,7},{5,8},{6,9},{7,10},{8,11},{9,12},{10... | collective-permute-start | bytes 786440 | tf_op jit(solution)/shard_map/ppermute | solution.py:41
  142.5 22.1 %collective-permute-start.15 = (bf16[1,128,16,64]{1,3,2,0:T(8,128)(2,1)S(1)}, bf16[1,128,16,64]{1,3,2,0:T(8,128)(2,1)S(1)}, u32[]{:S(2)}, u32[]{:S(2)}) collective-permute-start(bf16[1,128,16,64]{1,3,2,0:T(8,128)(2,1)S(1)} %pad_maximum_fusion.7), channel_id=1, source_target_pairs={{0,13},{1,14},{2,15},{3,0},{4,1},{5,2},{6,3},{7,4},{8,5},{9,6},{10... | collective-permute-start | bytes 786440 | tf_op jit(solution)/shard_map/ppermute | solution.py:41
  149.4 15.2 %collective-permute-start.16 = (bf16[1,128,16,64]{1,3,2,0:T(8,128)(2,1)S(1)}, bf16[1,128,16,64]{1,3,2,0:T(8,128)(2,1)S(1)}, u32[]{:S(2)}, u32[]{:S(2)}) collective-permute-start(bf16[1,128,16,64]{1,3,2,0:T(8,128)(2,1)S(1)} %pad_maximum_fusion.8), channel_id=1, source_target_pairs={{0,4},{1,5},{2,6},{3,7},{4,8},{5,9},{6,10},{7,11},{8,12},{9,13},{1... | collective-permute-start | bytes 786440 | tf_op jit(solution)/shard_map/ppermute | solution.py:41
  151.4 13.3 %collective-permute-start.17 = (bf16[1,128,16,64]{1,3,2,0:T(8,128)(2,1)S(1)}, bf16[1,128,16,64]{1,3,2,0:T(8,128)(2,1)S(1)}, u32[]{:S(2)}, u32[]{:S(2)}) collective-permute-start(bf16[1,128,16,64]{1,3,2,0:T(8,128)(2,1)S(1)} %pad_maximum_fusion.9), channel_id=1, source_target_pairs={{0,12},{1,13},{2,14},{3,15},{4,0},{5,1},{6,2},{7,3},{8,4},{9,5},{1... | collective-permute-start | bytes 786440 | tf_op jit(solution)/shard_map/ppermute | solution.py:41
  164.7 0.8 copy-start.15
  166.5 4.9 copy-start.13
  172.6 16.3 %collective-permute-start.19 = (bf16[1,64,1]{2,1,0:T(8,128)(2,1)}, bf16[1,64,1]{2,1,0:T(8,128)(2,1)S(1)}, u32[]{:S(2)}, u32[]{:S(2)}) collective-permute-start(bf16[1,64,1]{2,1,0:T(8,128)(2,1)} %get-tuple-element.37), channel_id=1, source_target_pairs={{0,1},{1,2},{2,3},{3,4},{4,5},{5,6},{6,7},{7,8},{8,9},{9,10},{10,1... | collective-permute-start | bytes 392 | tf_op jit(solution)/shard_map/ppermute | solution.py:29
  182.0 7.2 %collective-permute-start.18 = (bf16[1,64,1]{2,1,0:T(8,128)(2,1)}, bf16[1,64,1]{2,1,0:T(8,128)(2,1)S(1)}, u32[]{:S(2)}, u32[]{:S(2)}) collective-permute-start(bf16[1,64,1]{2,1,0:T(8,128)(2,1)} %get-tuple-element.36), channel_id=1, source_target_pairs={{1,0},{2,1},{3,2},{4,3},{5,4},{6,5},{7,6},{8,7},{9,8},{10,9},{11,1... | collective-permute-start | bytes 392 | tf_op jit(solution)/shard_map/ppermute | solution.py:31
  185.8 3.1 copy-start.7
  185.8 3.3 copy-start.11
  185.8 3.6 copy-start.3
  185.8 3.6 copy-start.18
  188.9 1.5 copy-start.10
  190.4 2.5 copy-start.8
  190.4 2.5 copy-start.16
  193.7 423.3 %all-reduce.9.cloned.1.call-start = ((), (), s32[]{:S(2)}) async-start(), calls=%async_computation.1 | async-start | bytes 630784
Sparse Core Ops, SparseCore 0:
  193.8 250.7 all-reduce.6
  448.4 168.5 all-reduce.8
